TPU v7x, 128 devices: a whole 4x4x4 slice. The times are simulated.
128 devices in a mesh: dp: 64 (over z, y, x), fsdp: 2 (over core).
Axes of the slice: x: 4, y: 4, z: 4, core: 2. Of those that a mesh axis runs over, the one named last changes fastest.
Arguments:
- mel_panels: bfloat16 [8192, 10240], P(('dp', 'fsdp')), may hold values from -6 to 6
- frames: int32 [8192], P(('dp', 'fsdp')), may hold values from 0 to 128, as said below
- target: int32 [8192], P(('dp', 'fsdp')), may hold values from 0 to 63, as said below
- conv_first: bfloat16 [9, 256], P(None, 'fsdp'), may hold values from -2 to 2
- depth_a: bfloat16 [9, 256], P(None, 'fsdp'), may hold values from -3 to 3
- point_a: bfloat16 [256, 256], P(None, 'fsdp'), may hold values from -0.5 to 0.5
- depth_b: bfloat16 [9, 256], P(None, 'fsdp'), may hold values from -3 to 3
- point_b: bfloat16 [256, 256], P(None, 'fsdp'), may hold values from -0.5 to 0.5
- linear_weight: bfloat16 [2560, 1024], P(None, 'fsdp'), may hold values from -0.15625 to 0.15625
- norm_gain: bfloat16 [1024], P('fsdp'), may hold values from 0.099609375 to 1.8984375
- up_weight: bfloat16 [1024, 2048], P(None, 'fsdp'), may hold values from -0.1875 to 0.1875
- depth_kernel: bfloat16 [9, 1024], P(None, 'fsdp'), may hold values from -2 to 2
- conv_gain: bfloat16 [1024], P('fsdp'), may hold values from 0.099609375 to 1.8984375
- down_weight: bfloat16 [1024, 1024], P('fsdp'), may hold values from -0.1875 to 0.1875
- cotangent: bfloat16 [65536, 1024], P(('dp', 'fsdp')), may hold values from -6 to 6
Outputs:
- layer_out: bfloat16 [65536, 1024], P(('dp', 'fsdp'))
- grad_input: bfloat16 [65536, 1024], P(('dp', 'fsdp'))
- grad_down: float32 [1024, 1024], P('fsdp')
Inputs may be any that keep to these rules, and one draw needn't show every extreme that they name: The slots of one loader are those of one index of dp and fsdp. A live slot holds a panel of 8 * m frames with 8 * m >= 32; frames = 0 marks an empty slot. Every device receives exactly 32 panels from the loaders of its own fsdp index, at most one from any loader, and one of them has 128 frames. `target`: only live slots are sent.
All inputs are finite; a program needn't handle non-finite values.
Results may differ from a plain program's by a relative error of at most 0.017.
Values may be sent and summed in bfloat16 or wider, within the bound.
A program may use at most 192 MiB of HBM per device.

v0:
```python
import math
import jax
import jax.numpy as jnp
from jax import lax
from jax.sharding import PartitionSpec as P

MELS = 80
PANEL = 128
EPSILON = 1e-05


def sent_together(arrays, axis, dim, along):
    widths = [a.shape[along] for a in arrays]
    both = jnp.concatenate(arrays, axis=along)
    out = lax.all_gather(both, axis, axis=dim, tiled=True)
    return tuple(jnp.split(out, [sum(widths[:k]) for k in range(1, len(widths))], axis=along))


def in_order(tiles, dim):
    dims = list(tiles.shape[1:])
    dims[dim] *= tiles.shape[0]
    return jnp.moveaxis(tiles, 0, dim).reshape(dims)


def gather_together(arrays, axis, dims):
    line = jnp.concatenate([a.reshape(-1) for a in arrays])
    lines, at, done = (lax.all_gather(line, axis), 0, [])
    for a, dim in zip(arrays, dims):
        tiles = lines[:, at : at + a.size].reshape(-1, *a.shape)
        done.append(in_order(tiles, dim))
        at += a.size
    return tuple(done)


def in_blocks(value, dim, size):
    before, after = (value.shape[:dim], value.shape[dim + 1 :])
    return jnp.moveaxis(value.reshape(*before, size, -1, *after), dim, 0)


def sent_and_summed(value, axis, dim):
    size = lax.axis_size(axis)
    tiles = lax.all_to_all(in_blocks(value, dim, size), axis, 0, 0, tiled=True)
    return jnp.sum(tiles.astype(jnp.float32), axis=0)


def phase_rows(source):
    shape_in = source.shape
    split = source.reshape((shape_in[0], shape_in[1] // 2, 2) + shape_in[2:])
    even = split[:, :, 0]
    odd = split[:, :, 1]
    before = jnp.concatenate([jnp.zeros_like(odd[:, :1]), odd[:, :-1]], axis=1)
    return (before, even, odd)


def phase_cols(source):
    shape_in = source.shape
    split = source.reshape(shape_in[:2] + (shape_in[2] // 2, 2) + shape_in[3:])
    even = split[:, :, :, 0]
    odd = split[:, :, :, 1]
    before = jnp.concatenate([jnp.zeros_like(odd[:, :, :1]), odd[:, :, :-1]], axis=2)
    return (before, even, odd)


def first_section(masked, weights):
    height = masked.shape[1] // 2
    breadth = masked.shape[2] // 2
    summed = jnp.zeros((masked.shape[0], height, breadth, weights.shape[1]), jnp.float32)
    row_views = phase_rows(masked)
    for i in range(3):
        col_views = phase_cols(row_views[i])
        for j in range(3):
            window = col_views[j].astype(jnp.float32)
            summed = summed + window[:, :, :, None] * weights[3 * i + j].astype(jnp.float32)
    return jnp.maximum(summed, 0.0).astype(jnp.bfloat16)


def depth_stride(source, weights):
    height = source.shape[1] // 2
    breadth = source.shape[2] // 2
    summed = jnp.zeros((source.shape[0], height, breadth, source.shape[3]), jnp.float32)
    row_views = phase_rows(source)
    for i in range(3):
        col_views = phase_cols(row_views[i])
        for j in range(3):
            window = col_views[j].astype(jnp.float32)
            summed = summed + window * weights[3 * i + j].astype(jnp.float32)
    return summed.astype(jnp.bfloat16)


def point_relu(spread, weights):
    shape_in = spread.shape
    mapped = jnp.dot(spread.reshape(-1, shape_in[3]), weights, preferred_element_type=jnp.float32)
    return jnp.maximum(mapped, 0.0).astype(jnp.bfloat16).reshape(shape_in[:3] + (weights.shape[1],))


def subsample(block_panels, block_lengths, conv_first, depth_a, point_a, depth_b, point_b):
    number = block_panels.shape[0]
    frames_in = block_panels.reshape(number, PANEL, MELS)
    inside = jnp.arange(PANEL)[None, :] < block_lengths[:, None]
    masked = jnp.where(inside[:, :, None], frames_in, jnp.zeros_like(frames_in))
    first = first_section(masked, conv_first)
    second = point_relu(depth_stride(first, depth_a), point_a)
    fourth = point_relu(depth_stride(second, depth_b), point_b)
    return fourth.reshape(number * fourth.shape[1], fourth.shape[2] * fourth.shape[3])


def depth_forward(gated, kernel, span):
    groups_in = gated.shape[0] // span
    half_width = kernel.shape[0] // 2
    shaped = jnp.pad(gated.reshape(groups_in, span, -1), ((0, 0), (half_width, half_width), (0, 0)))
    summed = jnp.zeros((groups_in, span, gated.shape[1]), jnp.float32)
    for k in range(kernel.shape[0]):
        summed = summed + shaped[:, k : k + span].astype(jnp.float32) * kernel[k].astype(
            jnp.float32
        )
    return summed.reshape(gated.shape[0], -1)


def depth_backward(upstream, kernel, span):
    groups_in = upstream.shape[0] // span
    half_width = kernel.shape[0] // 2
    shaped = jnp.pad(
        upstream.reshape(groups_in, span, -1), ((0, 0), (half_width, half_width), (0, 0))
    )
    summed = jnp.zeros((groups_in, span, upstream.shape[1]), jnp.float32)
    for k in range(kernel.shape[0]):
        offset = 2 * half_width - k
        summed = summed + shaped[:, offset : offset + span] * kernel[k].astype(jnp.float32)
    return summed.reshape(upstream.shape[0], -1)


def module_pass(
    features, keep, cotangent, norm_gain, up_weight, depth_kernel, conv_gain, down_weight, span
):
    width = features.shape[1]
    values = features.astype(jnp.float32)
    centred = values - jnp.mean(values, axis=1, keepdims=True)
    scale_one = lax.rsqrt(jnp.mean(centred * centred, axis=1, keepdims=True) + EPSILON)
    standard = centred * scale_one
    normed = (standard * norm_gain.astype(jnp.float32)).astype(jnp.bfloat16)
    projected = jnp.dot(normed, up_weight, preferred_element_type=jnp.float32)
    value_half = projected[:, :width]
    gate_half = jax.nn.sigmoid(projected[:, width:])
    row_keep = keep[:, None]
    gated = (row_keep * value_half * gate_half).astype(jnp.bfloat16)
    depthwise = depth_forward(gated, depth_kernel, span)
    centred_two = depthwise - jnp.mean(depthwise, axis=1, keepdims=True)
    scale_two = lax.rsqrt(jnp.mean(centred_two * centred_two, axis=1, keepdims=True) + EPSILON)
    standard_two = centred_two * scale_two
    active = standard_two * conv_gain.astype(jnp.float32)
    swish_gate = jax.nn.sigmoid(active)
    hidden = (active * swish_gate).astype(jnp.bfloat16)
    mixed = jnp.dot(hidden, down_weight, preferred_element_type=jnp.float32)
    layer_out = (row_keep * (values + mixed)).astype(jnp.bfloat16)
    back_out = jnp.where(row_keep > 0, cotangent, jnp.zeros_like(cotangent))
    back_hidden = lax.dot_general(
        back_out, down_weight, (((1,), (1,)), ((), ())), preferred_element_type=jnp.float32
    )
    back_active = back_hidden * (swish_gate + active * swish_gate * (1.0 - swish_gate))
    gain_back = back_active * conv_gain.astype(jnp.float32)
    back_depth = scale_two * (
        gain_back
        - jnp.mean(gain_back, axis=1, keepdims=True)
        - standard_two * jnp.mean(gain_back * standard_two, axis=1, keepdims=True)
    )
    back_gated = row_keep * depth_backward(back_depth, depth_kernel, span)
    back_proj = jnp.concatenate(
        [back_gated * gate_half, back_gated * value_half * gate_half * (1.0 - gate_half)], axis=1
    ).astype(jnp.bfloat16)
    back_normed = lax.dot_general(
        back_proj, up_weight, (((1,), (1,)), ((), ())), preferred_element_type=jnp.float32
    )
    gain_front = back_normed * norm_gain.astype(jnp.float32)
    back_input = scale_one * (
        gain_front
        - jnp.mean(gain_front, axis=1, keepdims=True)
        - standard * jnp.mean(gain_front * standard, axis=1, keepdims=True)
    )
    grad_input = (back_out.astype(jnp.float32) + back_input).astype(jnp.bfloat16)
    return (layer_out, grad_input, hidden, back_out)


def local(
    mel_panels,
    frames,
    target,
    conv_first,
    depth_a,
    point_a,
    depth_b,
    point_b,
    linear_weight,
    norm_gain,
    up_weight,
    depth_kernel,
    conv_gain,
    down_weight,
    cotangent,
):
    groups = lax.axis_size("dp")
    members = lax.axis_size("fsdp")
    span = PANEL // 8
    panel_count = cotangent.shape[0] // span
    destinations = jnp.arange(groups, dtype=jnp.int32)
    selected = (target[None, :] == destinations[:, None]) & (frames[None, :] > 0)
    outgoing = jnp.dot(
        selected.astype(jnp.bfloat16), mel_panels, preferred_element_type=jnp.float32
    ).astype(jnp.bfloat16)
    sent_frames = jnp.sum(jnp.where(selected, frames[None, :], 0), axis=1)
    incoming, got_frames = (
        lax.all_to_all(outgoing, "dp", split_axis=0, concat_axis=0, tiled=True),
        lax.all_to_all(sent_frames, "dp", split_axis=0, concat_axis=0, tiled=True),
    )
    present = got_frames > 0
    position = jnp.cumsum(present.astype(jnp.int32)) - 1
    places = jnp.arange(panel_count, dtype=jnp.int32)
    placing = (position[None, :] == places[:, None]) & present[None, :]
    panels = jnp.dot(
        placing.astype(jnp.bfloat16), incoming, preferred_element_type=jnp.float32
    ).astype(jnp.bfloat16)
    lengths = jnp.sum(jnp.where(placing, got_frames[None, :], 0), axis=1).astype(jnp.int32)
    first_full, depth_one, point_one, depth_two, point_two, gain_front, kernel_full, gain_back = (
        *sent_together((conv_first, depth_a, point_a, depth_b, point_b), "fsdp", 1, 0),
        lax.all_gather(norm_gain, "fsdp", axis=0, tiled=True),
        lax.all_gather(depth_kernel, "fsdp", axis=1, tiled=True),
        lax.all_gather(conv_gain, "fsdp", axis=0, tiled=True),
    )
    per_block = math.gcd(panel_count, 16)

    def sub_block(block_args):
        return subsample(
            block_args[0], block_args[1], first_full, depth_one, point_one, depth_two, point_two
        )

    flat_rows = lax.map(
        sub_block,
        (
            panels.reshape(panel_count // per_block, per_block, -1),
            lengths.reshape(panel_count // per_block, per_block),
        ),
    )
    flat_rows = flat_rows.reshape(panel_count * span, -1)
    features = jnp.dot(
        flat_rows,
        lax.all_gather(linear_weight, "fsdp", axis=1, tiled=True),
        preferred_element_type=jnp.float32,
    ).astype(jnp.bfloat16)
    keep = (jnp.arange(span)[None, :] < (lengths // 8)[:, None]).reshape(-1).astype(jnp.float32)
    up_full, down_full = gather_together((up_weight, down_weight), "fsdp", (1, 0))
    layer_out, grad_input, hidden, back_out = module_pass(
        features, keep, cotangent, gain_front, up_full, kernel_full, gain_back, down_full, span
    )
    local_rows = sent_and_summed(
        lax.dot_general(
            hidden, back_out, (((0,), (0,)), ((), ())), preferred_element_type=jnp.float32
        ).astype(jnp.bfloat16),
        "fsdp",
        0,
    )
    summed = lax.psum(local_rows, "dp")
    grad_down = summed / jnp.sqrt(jnp.float32(cotangent.shape[0] * groups * members))
    return (layer_out, grad_input, grad_down)


def solution(mesh):
    placed = (
        P(("dp", "fsdp"), None),
        P(("dp", "fsdp")),
        P(("dp", "fsdp")),
        P(None, "fsdp"),
        P(None, "fsdp"),
        P(None, "fsdp"),
        P(None, "fsdp"),
        P(None, "fsdp"),
        P(None, "fsdp"),
        P("fsdp"),
        P(None, "fsdp"),
        P(None, "fsdp"),
        P("fsdp"),
        P("fsdp", None),
        P(("dp", "fsdp"), None),
    )
    return jax.shard_map(
        local,
        mesh=mesh,
        in_specs=placed,
        out_specs=(P(("dp", "fsdp"), None), P(("dp", "fsdp"), None), P("fsdp", None)),
        check_vma=False,
    )
```

profile of v0, /device:TPU:0, one launch (start us, length us, event | category | flops | bytes accessed | tf_op | source)
XLA Modules:
  0.0 737.0 jit_solution(10071461535330743551)
XLA Ops:
  10.0 11.8 %all-to-all-start = ((s32[64,1,1]{2,1,0:T(1,128)}), s32[64,1,1]{2,1,0:T(1,128)}, u32[]{:S(2)}, u32[]{:S(2)}) async-start(s32[64,1,1]{2,1,0:T(1,128)} %copy.218), calls=%async_computation | async-start | bytes 65536 | tf_op jit(solution)/shard_map/all_to_all | solution.py:212
  24.1 10.4 %pad_maximum_fusion = bf16[1572864]{0:T(1024)(128)(2,1)} fusion(bf16[524288]{0:T(1024)(128)(2,1)S(1)} %bitcast.397, bf16[1048576]{0:T(1024)(128)(2,1)S(1)} %bitcast.392), kind=kLoop, calls=%fused_computation.103 | loop fusion | flops 6291456 | bytes 6291456 | tf_op jit(solution)/shard_map/concatenate | solution.py:26
  51.2 10.1 %all-to-all-start.1 = ((bf16[64,2,5120]{2,1,0:T(2,128)(2,1)}), bf16[64,2,5120]{2,1,0:T(2,128)(2,1)S(1)}, u32[]{:S(2)}, u32[]{:S(2)}) async-start(bf16[64,2,5120]{2,1,0:T(2,128)(2,1)} %reshape.638), calls=%async_computation.1 | async-start | bytes 2621440 | tf_op jit(solution)/shard_map/all_to_all | solution.py:211
  65.3 18.0 %all-to-all-done.1 = bf16[64,2,5120]{2,1,0:T(2,128)(2,1)S(1)} async-done(((bf16[64,2,5120]{2,1,0:T(2,128)(2,1)}), bf16[64,2,5120]{2,1,0:T(2,128)(2,1)S(1)}, u32[]{:S(2)}, u32[]{:S(2)}) %all-to-all-start.1) | async-done | bytes 1310752 | tf_op jit(solution)/shard_map/all_to_all | solution.py:211
  90.4 445.1 %while.10 = (s32[]{:T(128)}, bf16[2,256,2560]{2,1,0:T(8,128)(2,1)}, s32[2,16]{1,0:T(2,128)S(1)}, bf16[2,16,10240]{2,1,0:T(8,128)(2,1)}, bf16[9,256]{1,0:T(8,128)...) while((s32[]{:T(128)}, bf16[2,256,2560]{2,1,0:T(8,128)(2,1)}, ...), condition=%wide.region_4.5_spmd, body=%wide.region_3.4_spmd.sunk | while | flops 1972519936 | bytes 356025408 | solution.py:235
  146.4 54.4 %maximum_convert_fusion.2 = bf16[16,32,2,40,256]{4,1,3,0,2:T(8,128)(2,1)} fusion(f32[256]{0:T(256)S(1)} %bitcast.422, f32[16,32,2,40]{1,3,0,2:T(8,128)S(1)} %copy.284, f32[256]{0:T(256)S(1)} %bitcast.423, f32[16,32,2,40]{1,3,0,2:T(8,128)} %copy.286, f32[256]{0:T(256)S(1)} %bitcast.424, f32[16,32,2,40]{1,3,0,2:T(8,128)S(1)} %copy.289, ...), kind=kLoop, calls=%fused_computation.clone.1 | loop fusion | flops 199229440 | bytes 22455296 | tf_op jit(solution)/shard_map/while/body/eval_jaxpr/convert_element_type | solution.py:74
  200.8 17.6 %slice_bitcast_fusion.22 = (bf16[16,32,40,256]{3,1,2,0:T(8,128)(2,1)}, bf16[16,32,1,40,256]{4,1,3,0,2:T(8,128)(2,1)S(1)}, bf16[16,32,1,40,256]{4,1,3,0,2:T(8,128)(2,1)}) fusion(bf16[16,32,2,40,256]{4,1,3,0,2:T(8,128)(2,1)} %maximum_convert_fusion.2), kind=kLoop, calls=%fused_computation.89.clone.1 | loop fusion | bytes 52428800 | tf_op jit(solution)/shard_map/while/body/eval_jaxpr/squeeze | solution.py:50
  218.4 8.7 %concatenate.77 = bf16[16,32,40,256]{3,1,2,0:T(8,128)(2,1)S(1)} pad(bf16[16,31,40,256]{3,1,2,0:T(8,128)(2,1)} %bitcast.367, bf16[]{:T(256)} %constant.45.clone.7..sunk), padding=0_0x1_0x0_0x0_0 | pad | bytes 20643842 | tf_op jit(solution)/shard_map/while/body/eval_jaxpr/concatenate | solution.py:51
  254.9 14.6 %fusion.121 = bf16[16,32,20,256]{3,1,2,0:T(8,128)(2,1)} fusion(bf16[16,32,20,2,256]{4,1,3,2,0:T(8,128)(2,1)} %bitcast.366, bf16[16,32,20,2,256]{4,1,3,2,0:T(8,128)(2,1)S(1)} %bitcast.364, bf16[16,32,20,2,256]{4,1,3,2,0:T(8,128)(2,1)S(1)} %bitcast.362, f32[256]{0:T(256)S(1)} %bitcast.410, f32[256]{0:T(256)S(1)} %bitcast.409, f32[256]{0:T(256)S(1)} %bitcast.408, ...), kind=kLoop, calls=%fused_computation.6.clone.1 | loop fusion | flops 70778880 | bytes 51651584 | tf_op jit(solution)/shard_map/while/body/eval_jaxpr/convert_element_type | solution.py:87
  269.5 8.9 %copy.307 = bf16[16,32,20,256]{3,2,1,0:T(8,128)(2,1)} copy(bf16[16,32,20,256]{3,1,2,0:T(8,128)(2,1)} %fusion.121) | data formatting | bytes 10485760 | tf_op jit(solution)/shard_map/while/body/eval_jaxpr/convert_element_type | solution.py:87
  278.4 9.0 %reshape.645 = bf16[10240,256]{1,0:T(8,128)(2,1)} reshape(bf16[16,32,20,256]{3,2,1,0:T(8,128)(2,1)} %copy.307) | data formatting | bytes 10485760 | tf_op jit(solution)/shard_map/while/body/eval_jaxpr/reshape | solution.py:92
  287.4 6.3 fusion.122
  293.6 8.9 %reshape.646 = bf16[16,16,2,20,256]{4,3,2,1,0:T(8,128)(2,1)} reshape(bf16[10240,256]{1,0:T(8,128)(2,1)} %fusion.122) | data formatting | bytes 10485760 | tf_op jit(solution)/shard_map/while/body/eval_jaxpr/reshape;while/body/eval_jaxpr/reshape | solution.py:48
  355.1 54.4 %maximum_convert_fusion.2 = bf16[16,32,2,40,256]{4,1,3,0,2:T(8,128)(2,1)} fusion(f32[256]{0:T(256)S(1)} %bitcast.422, f32[16,32,2,40]{1,3,0,2:T(8,128)S(1)} %copy.284, f32[256]{0:T(256)S(1)} %bitcast.423, f32[16,32,2,40]{1,3,0,2:T(8,128)} %copy.286, f32[256]{0:T(256)S(1)} %bitcast.424, f32[16,32,2,40]{1,3,0,2:T(8,128)S(1)} %copy.289, ...), kind=kLoop, calls=%fused_computation.clone.1 | loop fusion | flops 199229440 | bytes 22455296 | tf_op jit(solution)/shard_map/while/body/eval_jaxpr/convert_element_type | solution.py:74
  409.5 17.6 %slice_bitcast_fusion.22 = (bf16[16,32,40,256]{3,1,2,0:T(8,128)(2,1)}, bf16[16,32,1,40,256]{4,1,3,0,2:T(8,128)(2,1)S(1)}, bf16[16,32,1,40,256]{4,1,3,0,2:T(8,128)(2,1)}) fusion(bf16[16,32,2,40,256]{4,1,3,0,2:T(8,128)(2,1)} %maximum_convert_fusion.2), kind=kLoop, calls=%fused_computation.89.clone.1 | loop fusion | bytes 52428800 | tf_op jit(solution)/shard_map/while/body/eval_jaxpr/squeeze | solution.py:50
  427.1 8.7 %concatenate.77 = bf16[16,32,40,256]{3,1,2,0:T(8,128)(2,1)S(1)} pad(bf16[16,31,40,256]{3,1,2,0:T(8,128)(2,1)} %bitcast.367, bf16[]{:T(256)} %constant.45.clone.7..sunk), padding=0_0x1_0x0_0x0_0 | pad | bytes 20643842 | tf_op jit(solution)/shard_map/while/body/eval_jaxpr/concatenate | solution.py:51
  463.5 14.6 %fusion.121 = bf16[16,32,20,256]{3,1,2,0:T(8,128)(2,1)} fusion(bf16[16,32,20,2,256]{4,1,3,2,0:T(8,128)(2,1)} %bitcast.366, bf16[16,32,20,2,256]{4,1,3,2,0:T(8,128)(2,1)S(1)} %bitcast.364, bf16[16,32,20,2,256]{4,1,3,2,0:T(8,128)(2,1)S(1)} %bitcast.362, f32[256]{0:T(256)S(1)} %bitcast.410, f32[256]{0:T(256)S(1)} %bitcast.409, f32[256]{0:T(256)S(1)} %bitcast.408, ...), kind=kLoop, calls=%fused_computation.6.clone.1 | loop fusion | flops 70778880 | bytes 51651584 | tf_op jit(solution)/shard_map/while/body/eval_jaxpr/convert_element_type | solution.py:87
  478.2 8.9 %copy.307 = bf16[16,32,20,256]{3,2,1,0:T(8,128)(2,1)} copy(bf16[16,32,20,256]{3,1,2,0:T(8,128)(2,1)} %fusion.121) | data formatting | bytes 10485760 | tf_op jit(solution)/shard_map/while/body/eval_jaxpr/convert_element_type | solution.py:87
  487.1 9.0 %reshape.645 = bf16[10240,256]{1,0:T(8,128)(2,1)} reshape(bf16[16,32,20,256]{3,2,1,0:T(8,128)(2,1)} %copy.307) | data formatting | bytes 10485760 | tf_op jit(solution)/shard_map/while/body/eval_jaxpr/reshape | solution.py:92
  496.0 6.3 fusion.122
  502.3 8.9 %reshape.646 = bf16[16,16,2,20,256]{4,3,2,1,0:T(8,128)(2,1)} reshape(bf16[10240,256]{1,0:T(8,128)(2,1)} %fusion.122) | data formatting | bytes 10485760 | tf_op jit(solution)/shard_map/while/body/eval_jaxpr/reshape;while/body/eval_jaxpr/reshape | solution.py:48
  535.6 6.2 convert_reduce_fusion.1
  542.3 6.9 reshape.629
  610.5 116.3 %all-reduce.16.cloned.1.call-done = f32[512,1024]{1,0:T(8,128)} async-done(((f32[512,1024]{1,0:T(8,128)}), f32[512,1024]{1,0:T(8,128)}) %all-reduce.16.cloned.1.call-update) | async-done | bytes 2097168 | tf_op jit(solution)/shard_map/psum | solution.py:260
  (313 shorter events, 257.4 us)
Async XLA Ops:
  7.2 32.2 %copy-start = (bf16[64,10240]{1,0:T(8,128)(2,1)S(1)}, bf16[64,10240]{1,0:T(8,128)(2,1)}, u32[]{:S(2)}) copy-start(bf16[64,10240]{1,0:T(8,128)(2,1)} %param.17) | copy-start | bytes 3932164
  7.2 15.4 %copy-start.10 = (bf16[1024,1024]{1,0:T(8,128)(2,1)S(1)}, bf16[1024,1024]{1,0:T(8,128)(2,1)}, u32[]{:S(2)}) copy-start(bf16[1024,1024]{1,0:T(8,128)(2,1)} %param.27) | copy-start | bytes 6291460
  10.0 41.2 %all-to-all-start = ((s32[64,1,1]{2,1,0:T(1,128)}), s32[64,1,1]{2,1,0:T(1,128)}, u32[]{:S(2)}, u32[]{:S(2)}) async-start(s32[64,1,1]{2,1,0:T(1,128)} %copy.218), calls=%async_computation | async-start | bytes 65536 | tf_op jit(solution)/shard_map/all_to_all | solution.py:212
  21.8 513.8 %all-gather.6.cloned.1.call-start = ((), (), s32[]{:S(2)}) async-start(), calls=%async_computation.3 | async-start | bytes 7864320 | tf_op jit(solution)/shard_map/all_gather | solution.py:245
  22.6 519.7 %all-gather.8.cloned.1.call-start = ((), (), s32[]{:S(2)}) async-start(), calls=%async_computation.5 | async-start | bytes 9437184 | tf_op jit(solution)/shard_map/all_gather | solution.py:27
  34.5 4.8 copy-start.38
  34.5 4.8 copy-start.40
  35.4 4.4 copy-start.41
  35.4 6.3 copy-start.33
  35.4 8.8 %copy-start.42 = (bf16[512]{0:T(512)(128)(2,1)S(1)}, bf16[512]{0:T(512)(128)(2,1)}, u32[]{:S(2)}) copy-start(bf16[512]{0:T(512)(128)(2,1)} %param.29) | copy-start | bytes 3076
  51.2 32.1 %all-to-all-start.1 = ((bf16[64,2,5120]{2,1,0:T(2,128)(2,1)}), bf16[64,2,5120]{2,1,0:T(2,128)(2,1)S(1)}, u32[]{:S(2)}, u32[]{:S(2)}) async-start(bf16[64,2,5120]{2,1,0:T(2,128)(2,1)} %reshape.638), calls=%async_computation.1 | async-start | bytes 2621440 | tf_op jit(solution)/shard_map/all_to_all | solution.py:211
  61.3 665.5 %all-reduce.16.cloned.1.call-start = ((), (), s32[]{:S(2)}) async-start(), calls=%async_computation.4 | async-start | bytes 4194304 | tf_op jit(solution)/shard_map/psum | solution.py:260
  64.8 25.7 %copy-start.29 = (f32[512]{0:T(512)}, f32[512]{0:T(512)S(1)}, u32[]{:S(2)}) copy-start(f32[512]{0:T(512)S(1)} %reshape.619) | copy-start | bytes 6148
  111.0 5.2 copy-start.43
  111.1 143.8 %copy-start.16 = (bf16[9,256]{1,0:T(8,128)(2,1)}, bf16[9,256]{1,0:T(8,128)(2,1)S(1)}, u32[]{:S(2)}) copy-start(bf16[9,256]{1,0:T(8,128)(2,1)S(1)} %get-tuple-element.321) | copy-start | bytes 13828 | tf_op jit(solution)/shard_map/while
  319.7 5.2 copy-start.43
  319.7 143.8 %copy-start.16 = (bf16[9,256]{1,0:T(8,128)(2,1)}, bf16[9,256]{1,0:T(8,128)(2,1)S(1)}, u32[]{:S(2)}) copy-start(bf16[9,256]{1,0:T(8,128)(2,1)S(1)} %get-tuple-element.321) | copy-start | bytes 13828 | tf_op jit(solution)/shard_map/while
  541.8 22.5 %copy-start.7 = (bf16[512,1024]{1,0:T(8,128)(2,1)}, bf16[512,1024]{1,0:T(8,128)(2,1)S(1)}, u32[]{:S(2)}) copy-start(bf16[512,1024]{1,0:T(8,128)(2,1)S(1)} %get-tuple-element.146) | copy-start | bytes 3145732
  549.3 2.8 copy-start.4
  552.0 2.8 slice-start.2
  558.1 6.2 copy-start.32
  564.3 4.6 copy-start.30
  598.9 5.5 copy-start.15
  608.2 121.8 %copy-start.1 = (bf16[64,10240]{1,0:T(8,128)(2,1)S(1)}, bf16[64,10240]{1,0:T(8,128)(2,1)}, u32[]{:S(2)}) copy-start(bf16[64,10240]{1,0:T(8,128)(2,1)} %param.17) | copy-start | bytes 3932164
  (37 other events, 61.0 us)
Sparse Core Ops, SparseCore 0:
  24.3 19.1 all-gather.5
  45.1 20.8 all-gather.7
  597.8 128.9 all-reduce.15
where the time goes:
time: 749 us; the launch traced here: 737 us
  local copies, waits for them, and re-layouts  292 us (39%)
  other arithmetic  190 us (25%)
  waiting for transfers between devices  135 us (18%)
  matrix products  41.8 us (6%)
  loops' own time  28.4 us (4%)
  starting transfers between devices  22 us (3%)
  between operations  14.7 us (2%)
  blocking collectives  13.3 us (2%)
    psum x1, waiting for transfers between devices, local(): summed = lax.psum(local_rows, 'dp')  116 us
    convert_element_type x2, other arithmetic, first_section(): return jnp.maximum(summed, 0.0).astype(jnp.bfloat16)  109 us
    mul x36, local copies, waits for them, and re-layouts, first_section(): window[:, :, :, None] * weights[3 * i + j].astype(jnp.float32)  46.2 us
    squeeze x4, local copies, waits for them, and re-layouts, phase_rows(): odd = split[:, :, 1]  42.2 us
    slice x16, local copies, waits for them, and re-layouts, phase_cols(): odd[:, :, :-1]  34.4 us
    convert_element_type x4, other arithmetic, depth_stride(): return summed.astype(jnp.bfloat16)  33.9 us
    another operation x1, loops' own time, local(): lax.map(sub_block, (panels.reshape(panel_count // per_block, per_block, -...  28.4 us
    squeeze x12, local copies, waits for them, and re-layouts, phase_cols(): odd = split[:, :, :, 1]  24.9 us
  transfers between devices with their start and end apart: 5, of which 2 were waited for; matrix products, arithmetic and copies ran while one was open for 62% of the time, Pallas kernels for 0%

commit v1 on v0

--- a/solution.py
+++ b/solution.py
@@ -257,7 +257,7 @@
         "fsdp",
         0,
     )
-    summed = lax.psum(local_rows, "dp")
+    summed = jnp.sum(lax.all_gather(local_rows, "dp"), axis=0)
     grad_down = summed / jnp.sqrt(jnp.float32(cotangent.shape[0] * groups * members))
     return (layer_out, grad_input, grad_down)
 

time: 749 us -> 1150 us (1.54)
  waiting for transfers between devices: 135 us -> 513 us
  other arithmetic: 190 us -> 226 us
    all_gather x0 -> x1, waiting for transfers between devices: none -> 493 us  [local(): summed = jnp.sum(lax.all_gather(local_rows, 'dp'), axis=0)]
    psum x1 -> x0, waiting for transfers between devices: 116 us -> none  [local(): summed = lax.psum(local_rows, 'dp')]
    reduce_sum x0 -> x1, other arithmetic: none -> 40.6 us  [local(): summed = jnp.sum(lax.all_gather(local_rows, 'dp'), axis=0)]
  transfers between devices with their start and end apart: 5 -> 5, of which waited for: 2 -> 2; matrix products, arithmetic and copies ran while one was open for 62% -> 39% of each run, Pallas kernels for 0% -> 0%
where the time goes in v1:
time: 1150 us; the launch traced here: 1140 us
  waiting for transfers between devices  513 us (45%)
  local copies, waits for them, and re-layouts  285 us (25%)
  other arithmetic  226 us (20%)
  matrix products  38.6 us (3%)
  loops' own time  30 us (3%)
  starting transfers between devices  22 us (2%)
  between operations  14.5 us (1%)
  blocking collectives  12.9 us (1%)
    all_gather x1, waiting for transfers between devices, local(): summed = jnp.sum(lax.all_gather(local_rows, 'dp'), axis=0)  493 us
    convert_element_type x2, other arithmetic, first_section(): return jnp.maximum(summed, 0.0).astype(jnp.bfloat16)  109 us
    mul x36, local copies, waits for them, and re-layouts, first_section(): window[:, :, :, None] * weights[3 * i + j].astype(jnp.float32)  46 us
    reduce_sum x1, other arithmetic, local(): summed = jnp.sum(lax.all_gather(local_rows, 'dp'), axis=0)  40.6 us
    slice x16, local copies, waits for them, and re-layouts, phase_cols(): odd[:, :, :-1]  37.6 us
    squeeze x4, local copies, waits for them, and re-layouts, phase_rows(): odd = split[:, :, 1]  35.2 us
    convert_element_type x4, other arithmetic, depth_stride(): return summed.astype(jnp.bfloat16)  33.9 us
    another operation x1, loops' own time, local(): lax.map(sub_block, (panels.reshape(panel_count // per_block, per_block, -...  30 us
  transfers between devices with their start and end apart: 5, of which 2 were waited for; matrix products, arithmetic and copies ran while one was open for 39% of the time, Pallas kernels for 0%

profile of v1, /device:TPU:0, one launch (start us, length us, event | category | flops | bytes accessed | tf_op | source)
XLA Modules:
  0.0 1141.9 jit_solution(11466798984186020646)
XLA Ops:
  8.8 11.5 %all-to-all-start = ((s32[64,1,1]{2,1,0:T(1,128)}), s32[64,1,1]{2,1,0:T(1,128)S(1)}, u32[]{:S(2)}, u32[]{:S(2)}) async-start(s32[64,1,1]{2,1,0:T(1,128)} %copy.218), calls=%async_computation | async-start | bytes 65536 | tf_op jit(solution)/shard_map/all_to_all | solution.py:212
  22.7 10.4 pad_maximum_fusion
  49.5 10.3 all-to-all-start.1
  62.3 19.6 %all-to-all-done.1 = bf16[64,2,5120]{2,1,0:T(2,128)(2,1)S(1)} async-done(((bf16[64,2,5120]{2,1,0:T(2,128)(2,1)}), bf16[64,2,5120]{2,1,0:T(2,128)(2,1)S(1)}, u32[]{:S(2)}, u32[]{:S(2)}) %all-to-all-start.1) | async-done | bytes 1310752 | tf_op jit(solution)/shard_map/all_to_all | solution.py:211
  88.9 434.0 %while.10 = (s32[]{:T(128)}, bf16[2,256,2560]{2,1,0:T(8,128)(2,1)}, s32[2,16]{1,0:T(2,128)S(1)}, bf16[2,16,10240]{2,1,0:T(8,128)(2,1)}, bf16[9,256]{1,0:T(8,128)...) while((s32[]{:T(128)}, bf16[2,256,2560]{2,1,0:T(8,128)(2,1)}, ...), condition=%wide.region_4.5_spmd, body=%wide.region_3.4_spmd.sunk | while | flops 1972519936 | bytes 399062016 | solution.py:235
  142.7 54.4 %maximum_convert_fusion.2 = bf16[16,32,2,40,256]{4,1,3,0,2:T(8,128)(2,1)} fusion(f32[256]{0:T(256)S(1)} %bitcast.423, f32[16,32,2,40]{1,3,0,2:T(8,128)S(1)} %copy.284, f32[256]{0:T(256)S(1)} %bitcast.424, f32[16,32,2,40]{1,3,0,2:T(8,128)} %copy.286, f32[256]{0:T(256)S(1)} %bitcast.425, f32[16,32,2,40]{1,3,0,2:T(8,128)S(1)} %copy.289, ...), kind=kLoop, calls=%fused_computation.clone.1 | loop fusion | flops 199229440 | bytes 22455296 | tf_op jit(solution)/shard_map/while/body/eval_jaxpr/convert_element_type | solution.py:74
  197.0 14.2 %slice_bitcast_fusion.22 = (bf16[16,32,40,256]{3,1,2,0:T(8,128)(2,1)}, bf16[16,32,1,40,256]{4,1,3,0,2:T(8,128)(2,1)S(1)}, bf16[16,32,1,40,256]{4,1,3,0,2:T(8,128)(2,1)S(1)}) fusion(bf16[16,32,2,40,256]{4,1,3,0,2:T(8,128)(2,1)} %maximum_convert_fusion.2), kind=kLoop, calls=%fused_computation.89.clone.1 | loop fusion | bytes 52428800 | tf_op jit(solution)/shard_map/while/body/eval_jaxpr/squeeze | solution.py:50
  214.7 6.9 slice.621
  230.0 8.7 concatenate.77
  247.2 14.6 %fusion.121 = bf16[16,32,20,256]{3,1,2,0:T(8,128)(2,1)} fusion(bf16[16,32,20,2,256]{4,1,3,2,0:T(8,128)(2,1)} %bitcast.367, bf16[16,32,20,2,256]{4,1,3,2,0:T(8,128)(2,1)S(1)} %bitcast.365, bf16[16,32,20,2,256]{4,1,3,2,0:T(8,128)(2,1)S(1)} %bitcast.363, f32[256]{0:T(256)S(1)} %bitcast.411, f32[256]{0:T(256)S(1)} %bitcast.410, f32[256]{0:T(256)S(1)} %bitcast.409, ...), kind=kLoop, calls=%fused_computation.6.clone.1 | loop fusion | flops 70778880 | bytes 51651584 | tf_op jit(solution)/shard_map/while/body/eval_jaxpr/convert_element_type | solution.py:87
  261.8 8.9 copy.307
  270.7 9.0 reshape.646
  286.0 8.9 reshape.647
  345.1 54.4 %maximum_convert_fusion.2 = bf16[16,32,2,40,256]{4,1,3,0,2:T(8,128)(2,1)} fusion(f32[256]{0:T(256)S(1)} %bitcast.423, f32[16,32,2,40]{1,3,0,2:T(8,128)S(1)} %copy.284, f32[256]{0:T(256)S(1)} %bitcast.424, f32[16,32,2,40]{1,3,0,2:T(8,128)} %copy.286, f32[256]{0:T(256)S(1)} %bitcast.425, f32[16,32,2,40]{1,3,0,2:T(8,128)S(1)} %copy.289, ...), kind=kLoop, calls=%fused_computation.clone.1 | loop fusion | flops 199229440 | bytes 22455296 | tf_op jit(solution)/shard_map/while/body/eval_jaxpr/convert_element_type | solution.py:74
  399.5 14.2 %slice_bitcast_fusion.22 = (bf16[16,32,40,256]{3,1,2,0:T(8,128)(2,1)}, bf16[16,32,1,40,256]{4,1,3,0,2:T(8,128)(2,1)S(1)}, bf16[16,32,1,40,256]{4,1,3,0,2:T(8,128)(2,1)S(1)}) fusion(bf16[16,32,2,40,256]{4,1,3,0,2:T(8,128)(2,1)} %maximum_convert_fusion.2), kind=kLoop, calls=%fused_computation.89.clone.1 | loop fusion | bytes 52428800 | tf_op jit(solution)/shard_map/while/body/eval_jaxpr/squeeze | solution.py:50
  432.5 8.7 concatenate.77
  449.6 14.6 %fusion.121 = bf16[16,32,20,256]{3,1,2,0:T(8,128)(2,1)} fusion(bf16[16,32,20,2,256]{4,1,3,2,0:T(8,128)(2,1)} %bitcast.367, bf16[16,32,20,2,256]{4,1,3,2,0:T(8,128)(2,1)S(1)} %bitcast.365, bf16[16,32,20,2,256]{4,1,3,2,0:T(8,128)(2,1)S(1)} %bitcast.363, f32[256]{0:T(256)S(1)} %bitcast.411, f32[256]{0:T(256)S(1)} %bitcast.410, f32[256]{0:T(256)S(1)} %bitcast.409, ...), kind=kLoop, calls=%fused_computation.6.clone.1 | loop fusion | flops 70778880 | bytes 51651584 | tf_op jit(solution)/shard_map/while/body/eval_jaxpr/convert_element_type | solution.py:87
  464.3 8.9 copy.307
  473.2 9.0 reshape.646
  488.5 8.9 reshape.647
  529.7 7.0 reshape.629
  536.6 7.9 slice.352
  600.1 492.9 %all-gather.12.cloned.1.call-done = f32[32768,1024]{1,0:T(8,128)} async-done(((f32[512,1024]{1,0:T(8,128)}), f32[32768,1024]{1,0:T(8,128)}) %all-gather.12.cloned.1.call-update) | async-done | bytes 134217744 | tf_op jit(solution)/shard_map/all_gather | solution.py:260
  1093.1 40.6 %reduce_sum.119 = f32[512,1024]{1,0:T(8,128)S(1)} reduce(f32[64,512,1024]{2,1,0:T(8,128)} %bitcast.87, f32[]{:T(128)} %constant.69.clone.1), dimensions={0}, to_apply=%region_14.15 | reduce | flops 33030144 | bytes 136314880 | tf_op jit(solution)/shard_map/reduce_sum | solution.py:260
  (364 shorter events, 253.0 us)
Async XLA Ops:
  7.2 37.3 %copy-start = (bf16[64,10240]{1,0:T(8,128)(2,1)S(1)}, bf16[64,10240]{1,0:T(8,128)(2,1)}, u32[]{:S(2)}) copy-start(bf16[64,10240]{1,0:T(8,128)(2,1)} %param.17) | copy-start | bytes 3932164
  7.2 14.8 %copy-start.12 = (bf16[1024,1024]{1,0:T(8,128)(2,1)S(1)}, bf16[1024,1024]{1,0:T(8,128)(2,1)}, u32[]{:S(2)}) copy-start(bf16[1024,1024]{1,0:T(8,128)(2,1)} %param.27) | copy-start | bytes 6291460
  7.2 515.7 %all-gather.8.cloned.1.call-start = ((), (), s32[]{:S(2)}) async-start(), calls=%async_computation.3 | async-start | bytes 7864320 | tf_op jit(solution)/shard_map/all_gather | solution.py:245
  8.8 40.7 %all-to-all-start = ((s32[64,1,1]{2,1,0:T(1,128)}), s32[64,1,1]{2,1,0:T(1,128)S(1)}, u32[]{:S(2)}, u32[]{:S(2)}) async-start(s32[64,1,1]{2,1,0:T(1,128)} %copy.218), calls=%async_computation | async-start | bytes 65536 | tf_op jit(solution)/shard_map/all_to_all | solution.py:212
  20.3 509.3 %all-gather.10.cloned.1.call-start = ((), (), s32[]{:S(2)}) async-start(), calls=%async_computation.4 | async-start | bytes 9437184 | tf_op jit(solution)/shard_map/all_gather | solution.py:27
  33.1 7.1 copy-start.52
  33.1 8.9 copy-start.45
  49.5 32.3 %all-to-all-start.1 = ((bf16[64,2,5120]{2,1,0:T(2,128)(2,1)}), bf16[64,2,5120]{2,1,0:T(2,128)(2,1)S(1)}, u32[]{:S(2)}, u32[]{:S(2)}) async-start(bf16[64,2,5120]{2,1,0:T(2,128)(2,1)} %reshape.639), calls=%async_computation.1 | async-start | bytes 2621440 | tf_op jit(solution)/shard_map/all_to_all | solution.py:211
  59.9 1033.2 %all-gather.12.cloned.1.call-start = ((), (), s32[]{:S(2)}) async-start(), calls=%async_computation.5 | async-start | bytes 136314880 | tf_op jit(solution)/shard_map/all_gather | solution.py:260
  61.8 27.1 %copy-start.41 = (f32[512]{0:T(512)}, f32[512]{0:T(512)S(1)}, u32[]{:S(2)}) copy-start(f32[512]{0:T(512)S(1)} %reshape.619) | copy-start | bytes 6148
  109.6 5.6 copy-start.17
  134.2 8.5 copy-start.28
  134.2 8.5 copy-start.29
  211.2 10.4 copy-start.2
  270.7 9.0 copy-start.7
  312.1 5.6 copy-start.17
  336.6 8.5 copy-start.28
  336.6 8.5 copy-start.29
  413.7 10.4 copy-start.2
  473.2 9.0 copy-start.7
  529.2 30.3 %copy-start.10 = (bf16[512,1024]{1,0:T(8,128)(2,1)}, bf16[512,1024]{1,0:T(8,128)(2,1)S(1)}, u32[]{:S(2)}) copy-start(bf16[512,1024]{1,0:T(8,128)(2,1)S(1)} %get-tuple-element.146) | copy-start | bytes 3145732
  536.6 7.9 slice-start.2
  553.3 6.2 copy-start.43
  1093.1 42.1 %copy-start.1 = (bf16[64,10240]{1,0:T(8,128)(2,1)S(1)}, bf16[64,10240]{1,0:T(8,128)(2,1)}, u32[]{:S(2)}) copy-start(bf16[64,10240]{1,0:T(8,128)(2,1)} %param.17) | copy-start | bytes 3932164
  (62 other events, 107.3 us)
Sparse Core Ops, SparseCore 0:
  9.7 20.3 all-gather.7
  33.2 20.7 all-gather.9
  584.3 508.7 all-gather.11
